TPU v7x, 32 devices: a whole 2x2x4 slice. The times are simulated.
32 devices in a mesh: dp: 8 (over z, x), mp: 4 (over y, core).
Axes of the slice: x: 2, y: 2, z: 4, core: 2. Of those that a mesh axis runs over, the one named last changes fastest.
Arguments:
- tokens: bfloat16 [2, 16384, 768], P(None, ('dp', 'mp')), may hold values from -6 to 6
- norm_gains: bfloat16 [768, 2], P('dp'), may hold values from 0.5 to 1.5
- norm_biases: bfloat16 [768, 2], P('dp'), may hold values from -3 to 3
- w_query: bfloat16 [768, 768], P('dp', 'mp'), may hold values from -0.21875 to 0.21875
- w_keyval: bfloat16 [768, 128], P('dp'), may hold values from -0.21875 to 0.21875
- w_output: bfloat16 [768, 768], P('dp', 'mp'), may hold values from -1.5 to 1.5
- w_up: bfloat16 [768, 3072], P('dp', 'mp'), may hold values from -0.21875 to 0.21875
- w_down: bfloat16 [768, 3072], P('dp', 'mp'), may hold values from -0.109375 to 0.109375
- cotangent: bfloat16 [2, 16384, 768], P(None, ('dp', 'mp')), may hold values from -6 to 6
- subset_ids: int32 [32768], P('dp'), may hold values from 0 to 21
- subset_weights: float32 [22], replicated, may hold values from 0.25 to 4
Outputs:
- output: bfloat16 [2, 16384, 768], P(None, ('dp', 'mp'))
- kv_cache: bfloat16 [32768, 128], P('dp')
- input_grad: bfloat16 [2, 16384, 768], P(None, ('dp', 'mp'))
- grad_gains: float32 [768, 2], P('dp')
- grad_biases: float32 [768, 2], P('dp')
- grad_query: float32 [768, 768], P('dp', 'mp')
- grad_keyval: float32 [768, 128], P('dp')
- grad_output: float32 [768, 768], P('dp', 'mp')
- grad_up: float32 [768, 3072], P('dp', 'mp')
- grad_down: float32 [768, 3072], P('dp', 'mp')
All inputs are finite; a program needn't handle non-finite values.
Results may differ from a plain program's by a relative error of at most 0.012.
Values may be sent and summed in bfloat16 or wider, within the bound.
A program may use at most 256 MiB of HBM per device.

v0:
```python
import jax
import jax.numpy as jnp
from jax import lax
from jax.sharding import PartitionSpec as P

HD = 64
ROT = 16
SEQ_LEN = 2048
QB = 512
epsilon = 1e-05
sqrt_half = 0.7071067811865476
inv_sqrt_two_pi = 0.3989422804014327


def rotary_tables():
    position = jnp.arange(SEQ_LEN, dtype=jnp.float32)
    frequency = 10000.0 ** (-2.0 * jnp.arange(ROT // 2, dtype=jnp.float32) / ROT)
    angles = position[:, None] * frequency[None, :]
    return (jnp.cos(angles), jnp.sin(angles))


def rotate(vectors, cosine, sine_table):
    first_half = vectors[..., : ROT // 2]
    second_half = vectors[..., ROT // 2 : ROT]
    cos_wide = cosine[:, None, :]
    sin_wide = sine_table[:, None, :]
    return jnp.concatenate(
        [
            first_half * cos_wide - second_half * sin_wide,
            second_half * cos_wide + first_half * sin_wide,
            vectors[..., ROT:],
        ],
        axis=-1,
    )


def causal_scores(query_block, key_rows, row_begin, finish):
    scores = jnp.einsum(
        "sqhd,skd->shqk", query_block, key_rows[:, :finish], preferred_element_type=jnp.float32
    )
    row_ids = row_begin + jnp.arange(QB, dtype=jnp.int32)
    col_ids = jnp.arange(finish, dtype=jnp.int32)
    causal = col_ids[None, :] <= row_ids[:, None]
    return jnp.where(causal, scores, -1e30)


def attention_forward(queries, key_rows, value_rows):
    blocks = SEQ_LEN // QB
    pieces = []
    log_norms = []
    for block_index in range(blocks):
        row_begin = block_index * QB
        finish = row_begin + QB
        scores = causal_scores(queries[:, row_begin:finish], key_rows, row_begin, finish)
        maximum = jnp.max(scores, axis=-1, keepdims=True)
        shifted = jnp.exp(scores - maximum)
        totals = jnp.sum(shifted, axis=-1, keepdims=True)
        probability = (shifted / totals).astype(jnp.bfloat16)
        pieces.append(
            jnp.einsum(
                "shqk,skd->sqhd",
                probability,
                value_rows[:, :finish],
                preferred_element_type=jnp.float32,
            )
        )
        log_norms.append(maximum + jnp.log(totals))
    return (jnp.concatenate(pieces, axis=1), log_norms)


def attention_backward(queries, key_rows, value_rows, log_norms, grad_heads):
    blocks = SEQ_LEN // QB
    length = key_rows.shape[1]
    query_pieces = []
    grad_keys = jnp.zeros(key_rows.shape, jnp.float32)
    grad_values = jnp.zeros(value_rows.shape, jnp.float32)
    for block_index in range(blocks):
        row_begin = block_index * QB
        finish = row_begin + QB
        query_block = queries[:, row_begin:finish]
        grad_block = grad_heads[:, row_begin:finish]
        scores = causal_scores(query_block, key_rows, row_begin, finish)
        probability = jnp.exp(scores - log_norms[block_index])
        grad_probs = jnp.einsum(
            "sqhd,skd->shqk", grad_block, value_rows[:, :finish], preferred_element_type=jnp.float32
        )
        inner_sum = jnp.sum(probability * grad_probs, axis=-1, keepdims=True)
        grad_scores = (probability * (grad_probs - inner_sum)).astype(jnp.bfloat16)
        query_pieces.append(
            jnp.einsum(
                "shqk,skd->sqhd",
                grad_scores,
                key_rows[:, :finish],
                preferred_element_type=jnp.float32,
            )
        )
        key_part = jnp.einsum(
            "shqk,sqhd->skd", grad_scores, query_block, preferred_element_type=jnp.float32
        )
        value_part = jnp.einsum(
            "shqk,sqhd->skd",
            probability.astype(jnp.bfloat16),
            grad_block,
            preferred_element_type=jnp.float32,
        )
        padding = ((0, 0), (0, length - finish), (0, 0))
        grad_keys = grad_keys + jnp.pad(key_part, padding)
        grad_values = grad_values + jnp.pad(value_part, padding)
    return (jnp.concatenate(query_pieces, axis=1), grad_keys, grad_values)


def shards(
    tokens,
    norm_gains,
    norm_biases,
    w_query,
    w_keyval,
    w_output,
    w_up,
    w_down,
    cotangent,
    subset_ids,
    subset_weights,
):
    micro_count = tokens.shape[0]
    own_rows = tokens.shape[1]
    micro_rows = subset_ids.shape[0] // micro_count
    sequences = micro_rows // SEQ_LEN
    head_count = w_query.shape[1] // HD
    kv_share = 1.0 / lax.axis_size("mp")
    own_begin = lax.axis_index("mp") * own_rows
    cosine, sine_table = rotary_tables()
    matches = subset_ids[:, None] == jnp.arange(subset_weights.shape[0], dtype=jnp.int32)[None, :]
    row_scale = jnp.sum(jnp.where(matches, subset_weights[None, :], 0.0), axis=1)
    outputs = []
    caches = []
    input_grads = []
    summed = None
    for micro_index in range(micro_count):
        row_begin = micro_index * micro_rows
        rows_in = tokens[micro_index]
        cot_rows = cotangent[micro_index]
        scale_rows = row_scale[row_begin : row_begin + micro_rows]
        own_scale = lax.dynamic_slice_in_dim(scale_rows, own_begin, own_rows, 0)
        gathered = (
            lax.all_gather(norm_gains, "dp", axis=0, tiled=True),
            lax.all_gather(norm_biases, "dp", axis=0, tiled=True),
            lax.all_gather(w_query, "dp", axis=0, tiled=True),
            lax.all_gather(w_keyval, "dp", axis=0, tiled=True),
            lax.all_gather(w_output, "dp", axis=0, tiled=True),
            lax.all_gather(w_up, "dp", axis=0, tiled=True),
            lax.all_gather(w_down, "dp", axis=0, tiled=True),
        )
        gains_full, biases_full, query_w, keyval_w, output_w, up_w, down_w = gathered
        rows_full = lax.all_gather(rows_in, "mp", axis=0, tiled=True).astype(jnp.float32)
        mean_row = jnp.mean(rows_full, axis=1, keepdims=True)
        centered = rows_full - mean_row
        inverse = lax.rsqrt(jnp.mean(centered * centered, axis=1, keepdims=True) + epsilon)
        normed = centered * inverse
        gains_float = gains_full.astype(jnp.float32)
        biases_float = biases_full.astype(jnp.float32)
        attn_in = (normed * gains_float[:, 0] + biases_float[:, 0]).astype(jnp.bfloat16)
        mlp_in = (normed * gains_float[:, 1] + biases_float[:, 1]).astype(jnp.bfloat16)
        query_pre = jnp.dot(attn_in, query_w, preferred_element_type=jnp.float32)
        keyval_pre = jnp.dot(attn_in, keyval_w, preferred_element_type=jnp.float32)
        queries = (
            rotate(query_pre.reshape(sequences, SEQ_LEN, head_count, HD), cosine, sine_table)
            * HD ** (-0.5)
        ).astype(jnp.bfloat16)
        key_rows = (
            rotate(keyval_pre[:, :HD].reshape(sequences, SEQ_LEN, 1, HD), cosine, sine_table)
            .astype(jnp.bfloat16)
            .reshape(sequences, SEQ_LEN, HD)
        )
        value_rows = keyval_pre[:, HD:].astype(jnp.bfloat16).reshape(sequences, SEQ_LEN, HD)
        caches.append(jnp.concatenate([key_rows, value_rows], axis=-1).reshape(micro_rows, 2 * HD))
        mixed_heads, log_norms = attention_forward(queries, key_rows, value_rows)
        heads_out = mixed_heads.reshape(micro_rows, head_count * HD).astype(jnp.bfloat16)
        hidden_pre = jnp.dot(mlp_in, up_w, preferred_element_type=jnp.float32)
        hidden = jax.nn.gelu(hidden_pre, approximate=False).astype(jnp.bfloat16)
        branch_sum = jnp.einsum(
            "rc,dc->rd", heads_out, output_w, preferred_element_type=jnp.float32
        ) + jnp.einsum("rf,df->rd", hidden, down_w, preferred_element_type=jnp.float32)
        reduced_out = lax.psum_scatter(branch_sum, "mp", scatter_dimension=0, tiled=True)
        outputs.append((reduced_out + rows_in.astype(jnp.float32)).astype(jnp.bfloat16))
        gathered_back = (
            lax.all_gather(norm_gains, "dp", axis=0, tiled=True),
            lax.all_gather(w_query, "dp", axis=0, tiled=True),
            lax.all_gather(w_keyval, "dp", axis=0, tiled=True),
            lax.all_gather(w_output, "dp", axis=0, tiled=True),
            lax.all_gather(w_up, "dp", axis=0, tiled=True),
            lax.all_gather(w_down, "dp", axis=0, tiled=True),
        )
        gains_back, query_back, keyval_back, output_back, up_back, down_back = gathered_back
        cot_full = lax.all_gather(cot_rows, "mp", axis=0, tiled=True).astype(jnp.float32)
        grad_low = (cot_full * scale_rows[:, None]).astype(jnp.bfloat16)
        grad_hidden = jnp.dot(grad_low, down_back, preferred_element_type=jnp.float32)
        normal_cdf = 0.5 * (1.0 + jax.scipy.special.erf(hidden_pre * sqrt_half))
        density = jnp.exp(-0.5 * hidden_pre * hidden_pre) * inv_sqrt_two_pi
        grad_hidden_pre = (grad_hidden * (normal_cdf + hidden_pre * density)).astype(jnp.bfloat16)
        grad_down = jnp.einsum("rd,rf->df", grad_low, hidden, preferred_element_type=jnp.float32)
        grad_up = jnp.einsum(
            "rd,rf->df", mlp_in, grad_hidden_pre, preferred_element_type=jnp.float32
        )
        grad_mlp_in = jnp.einsum(
            "rf,df->rd", grad_hidden_pre, up_back, preferred_element_type=jnp.float32
        )
        grad_heads = jnp.dot(grad_low, output_back, preferred_element_type=jnp.float32).astype(
            jnp.bfloat16
        )
        grad_output = jnp.einsum(
            "rd,rc->dc", grad_low, heads_out, preferred_element_type=jnp.float32
        )
        grad_queries, grad_keys, grad_values = attention_backward(
            queries,
            key_rows,
            value_rows,
            log_norms,
            grad_heads.reshape(sequences, SEQ_LEN, head_count, HD),
        )
        grad_query_pre = (
            (rotate(grad_queries, cosine, -sine_table) * HD ** (-0.5))
            .astype(jnp.bfloat16)
            .reshape(micro_rows, head_count * HD)
        )
        grad_query = jnp.einsum(
            "rd,rc->dc", attn_in, grad_query_pre, preferred_element_type=jnp.float32
        )
        grad_attn_query = jnp.einsum(
            "rc,dc->rd", grad_query_pre, query_back, preferred_element_type=jnp.float32
        )
        gain_part = jnp.stack(
            [jnp.sum(grad_attn_query * normed, axis=0), jnp.sum(grad_mlp_in * normed, axis=0)],
            axis=1,
        )
        bias_part = jnp.stack(
            [jnp.sum(grad_attn_query, axis=0), jnp.sum(grad_mlp_in, axis=0)], axis=1
        )
        keyval_part = jnp.concatenate([grad_keys, grad_values], axis=-1).reshape(micro_rows, 2 * HD)
        keyval_sum, gain_sum, bias_sum = lax.psum((keyval_part, gain_part, bias_part), "mp")
        grad_key_pre = rotate(
            keyval_sum[:, :HD].reshape(sequences, SEQ_LEN, 1, HD), cosine, -sine_table
        ).reshape(micro_rows, HD)
        grad_keyval_pre = jnp.concatenate([grad_key_pre, keyval_sum[:, HD:]], axis=1).astype(
            jnp.bfloat16
        )
        grad_keyval = jnp.einsum(
            "rd,rc->dc", attn_in, grad_keyval_pre, preferred_element_type=jnp.float32
        )
        grad_attn_keyval = jnp.einsum(
            "rc,dc->rd", grad_keyval_pre, keyval_back, preferred_element_type=jnp.float32
        )
        kv_gain = jnp.sum(grad_attn_keyval * normed, axis=0)
        kv_bias = jnp.sum(grad_attn_keyval, axis=0)
        grad_gains = gain_sum + jnp.stack([kv_gain, jnp.zeros_like(kv_gain)], axis=1)
        grad_biases = bias_sum + jnp.stack([kv_bias, jnp.zeros_like(kv_bias)], axis=1)
        grad_attn_in = grad_attn_query + kv_share * grad_attn_keyval
        gains_back_float = gains_back.astype(jnp.float32)
        grad_normed = grad_attn_in * gains_back_float[:, 0] + grad_mlp_in * gains_back_float[:, 1]
        centered_grad = (
            grad_normed
            - jnp.mean(grad_normed, axis=1, keepdims=True)
            - normed * jnp.mean(grad_normed * normed, axis=1, keepdims=True)
        )
        reduced_grad = lax.psum_scatter(
            centered_grad * inverse, "mp", scatter_dimension=0, tiled=True
        )
        local_rows = cot_rows.astype(jnp.float32) * own_scale[:, None]
        input_grads.append((reduced_grad + local_rows).astype(jnp.bfloat16))
        local_grads = (
            grad_gains,
            grad_biases,
            grad_query,
            grad_keyval,
            grad_output,
            grad_up,
            grad_down,
        )
        reduced = (
            lax.psum_scatter(local_grads[0], "dp", scatter_dimension=0, tiled=True),
            lax.psum_scatter(local_grads[1], "dp", scatter_dimension=0, tiled=True),
            lax.psum_scatter(local_grads[2], "dp", scatter_dimension=0, tiled=True),
            lax.psum_scatter(local_grads[3], "dp", scatter_dimension=0, tiled=True),
            lax.psum_scatter(local_grads[4], "dp", scatter_dimension=0, tiled=True),
            lax.psum_scatter(local_grads[5], "dp", scatter_dimension=0, tiled=True),
            lax.psum_scatter(local_grads[6], "dp", scatter_dimension=0, tiled=True),
        )
        summed = (
            reduced
            if summed is None
            else tuple((running + added for running, added in zip(summed, reduced)))
        )
    return (
        jnp.stack(outputs, axis=0),
        jnp.concatenate(caches, axis=0),
        jnp.stack(input_grads, axis=0),
        summed[0],
        summed[1],
        summed[2],
        summed[3],
        summed[4],
        summed[5],
        summed[6],
    )


def solution(mesh):
    return jax.shard_map(
        shards,
        mesh=mesh,
        in_specs=(
            P(None, ("dp", "mp"), None),
            P("dp", None),
            P("dp", None),
            P("dp", "mp"),
            P("dp", None),
            P("dp", "mp"),
            P("dp", "mp"),
            P("dp", "mp"),
            P(None, ("dp", "mp"), None),
            P("dp"),
            P(),
        ),
        out_specs=(
            P(None, ("dp", "mp"), None),
            P("dp", None),
            P(None, ("dp", "mp"), None),
            P("dp", None),
            P("dp", None),
            P("dp", "mp"),
            P("dp", None),
            P("dp", "mp"),
            P("dp", "mp"),
            P("dp", "mp"),
        ),
        check_vma=False,
    )
```

profile of v0, /device:TPU:0, one launch (start us, length us, event | category | flops | bytes accessed | tf_op | source)
XLA Modules:
  0.0 1251.4 jit_solution(10996470224705625093)
XLA Ops:
  15.4 22.3 %all-gather.4 = bf16[8,96,2]{1,2,0:T(2,128)(2,1)S(1)} all-gather(bf16[1,96,2]{1,2,0:T(2,128)(2,1)S(1)} %bitcast.1078), channel_id=1, replica_groups=mesh['dp'=8,'mp'=4] {'dp'}, dimensions={0}, use_global_device_ids=true | all-gather | bytes 3456 | tf_op jit(solution)/shard_map/all_gather | solution.py:146
  38.4 16.3 %all-gather.5 = bf16[8,96,2]{1,2,0:T(2,128)(2,1)S(1)} all-gather(bf16[1,96,2]{1,2,0:T(2,128)(2,1)S(1)} %bitcast.1079), channel_id=1, replica_groups=mesh['dp'=8,'mp'=4] {'dp'}, dimensions={0}, use_global_device_ids=true | all-gather | bytes 3456 | tf_op jit(solution)/shard_map/all_gather | solution.py:147
  55.5 32.6 %all_gather.25 = bf16[768,128]{1,0:T(8,128)(2,1)} all-gather(bf16[96,128]{1,0:T(8,128)(2,1)S(1)} %copy-done.158), channel_id=1, replica_groups=mesh['dp'=8,'mp'=4] {'dp'}, dimensions={0}, use_global_device_ids=true | all-gather | bytes 221184 | tf_op jit(solution)/shard_map/all_gather | solution.py:149
  89.1 33.2 %all_gather.26 = bf16[768,192]{1,0:T(8,128)(2,1)} all-gather(bf16[96,192]{1,0:T(8,128)(2,1)S(1)} %copy-done.148), channel_id=1, replica_groups=mesh['dp'=8,'mp'=4] {'dp'}, dimensions={0}, use_global_device_ids=true | all-gather | bytes 331776 | tf_op jit(solution)/shard_map/all_gather | solution.py:148
  122.3 33.3 %all_gather.27 = bf16[768,192]{1,0:T(8,128)(2,1)} all-gather(bf16[96,192]{1,0:T(8,128)(2,1)S(1)} %copy-done.149), channel_id=1, replica_groups=mesh['dp'=8,'mp'=4] {'dp'}, dimensions={0}, use_global_device_ids=true | all-gather | bytes 331776 | tf_op jit(solution)/shard_map/all_gather | solution.py:150
  235.2 6.4 fusion.142
  269.9 6.7 fusion.13
  281.6 11.7 fusion.126
  293.3 11.3 fusion.127
  317.4 6.3 fusion.281
  335.5 15.2 %fusion.3 = (f32[3,512]{1,0:T(4,128)}, f32[3,512]{1,0:T(4,128)}, f32[2048,512,3]{1,0,2:T(8,128)}) fusion(f32[2048,512,3]{1,0,2:T(8,128)} %copy-done.2, f32[3,512]{1,0:T(4,128)S(1)} %log_add_fusion.4, pred[512,2048]{0,1:T(8,128)(4,1)S(1)} %copy-done.7, f32[2048,512,3]{1,0,2:T(8,128)S(1)} %fusion.296, bf16[1,2048,3,64]{1,3,2,0:T(8,128)(2,1)} %bitcast.1072, ...), kind=kOutput, calls=%fused_computation.9 | convolution fusion | flops 421524480 | bytes 39274496 | tf_op jit(solution)/shard_map/sqhd,skd->shqk/dot_general | solution.py:84
  355.6 18.4 %fusion.84 = (bf16[3,512,2048]{1,2,0:T(8,128)(2,1)S(1)}, f32[3,512]{1,0:T(4,128)S(1)}) fusion(f32[2048,512,3]{1,0,2:T(8,128)} %get-tuple-element.174, f32[2048,512,3]{1,0,2:T(8,128)} %copy-done.2, f32[3,512]{1,0:T(4,128)} %get-tuple-element.76, f32[3,512]{1,0:T(4,128)} %copy-done.133, pred[512,2048]{0,1:T(8,128)(4,1)} %iota_compare_fusion, ...), kind=kLoop, calls=%fused_computation.116 | loop fusion | flops 28310016 | bytes 57696256 | tf_op jit(solution)/shard_map/reshape.130
  374.1 12.5 fusion.85
  418.9 7.1 fusion.253
  426.2 19.3 %fusion.68 = (bf16[2048,768]{1,0:T(8,128)(2,1)}, f32[2048,768]{1,0:T(8,128)}) fusion(bf16[768,768]{1,0:T(8,128)(2,1)} %all-gather.13.cloned.1.call-done, bf16[1,2048,768]{2,1,0:T(8,128)(2,1)} %all-gather.17.cloned.1.call-done, f32[768]{0:T(1024)S(1)} %copy-done.172, f32[768]{0:T(1024)S(1)} %copy-done.168, f32[2048]{0:T(1024)S(1)} %copy-done.144, ...), kind=kOutput, calls=%fused_computation.100 | convolution fusion | flops 2527592448 | bytes 13785088 | tf_op jit(solution)/shard_map/dot_general | solution.py:179
  445.6 17.8 %fusion.71 = (bf16[2048,768]{1,0:T(8,128)(2,1)}, f32[2048,768]{1,0:T(8,128)}) fusion(bf16[768,768]{1,0:T(8,128)(2,1)S(1)} %copy-done.180, bf16[1,2048,768]{2,1,0:T(8,128)(2,1)S(1)} %copy-done.16, f32[2048]{0:T(1024)S(1)} %copy-done.140, f32[2048]{0:T(1024)S(1)} %copy-done.127, f32[768]{0:T(1024)S(1)} %copy-done.172, f32[768]{0:T(1024)S(1)} %copy-done.168), kind=kOutput, calls=%fused_computation.103 | convolution fusion | flops 2527592448 | bytes 13785088 | tf_op jit(solution)/shard_map/dot_general | solution.py:179
  463.4 7.6 fusion.77
  500.0 11.5 fusion.357
  511.7 7.3 fusion.354
  519.2 10.3 all-reduce.16
  531.5 6.5 convolution_add_fusion.1
  568.4 6.3 fusion.38
  624.8 31.7 %reduce-scatter.36.cloned.1.call-done = f32[96,2]{1,0:T(8,128)} async-done(((f32[768,2]{1,0:T(8,128)}), f32[96,2]{1,0:T(8,128)}) %reduce-scatter.36.cloned.1.call-update) | async-done | bytes 784
  658.0 58.9 %reduce-scatter.16.cloned.1.call-done = f32[512,768]{1,0:T(8,128)} async-done(((f32[2048,768]{1,0:T(8,128)}), f32[512,768]{1,0:T(8,128)}) %reduce-scatter.16.cloned.1.call-update) | async-done | bytes 1572880 | tf_op jit(solution)/shard_map/reduce_scatter | solution.py:184
  716.8 61.4 %reduce-scatter.18.cloned.1.call-done = f32[512,768]{1,0:T(8,128)} async-done(((f32[2048,768]{1,0:T(8,128)}), f32[512,768]{1,0:T(8,128)}) %reduce-scatter.18.cloned.1.call-update) | async-done | bytes 1572880 | tf_op jit(solution)/shard_map/reduce_scatter | solution.py:184
  781.8 57.8 %reduce-scatter.22.cloned.1.call-done = f32[512,768]{1,0:T(8,128)} async-done(((f32[2048,768]{1,0:T(8,128)}), f32[512,768]{1,0:T(8,128)}) %reduce-scatter.22.cloned.1.call-update) | async-done | bytes 1572880 | tf_op jit(solution)/shard_map/reduce_scatter | solution.py:265
  839.6 61.4 %reduce-scatter.20.cloned.1.call-done = f32[512,768]{1,0:T(8,128)} async-done(((f32[2048,768]{1,0:T(8,128)}), f32[512,768]{1,0:T(8,128)}) %reduce-scatter.20.cloned.1.call-update) | async-done | bytes 1572880 | tf_op jit(solution)/shard_map/reduce_scatter | solution.py:265
  904.6 63.4 %reduce-scatter.28.cloned.1.call-done = f32[96,192]{1,0:T(8,128)} async-done(((f32[768,192]{1,0:T(8,128)}), f32[96,192]{1,0:T(8,128)}) %reduce-scatter.28.cloned.1.call-update) | async-done | bytes 73744 | tf_op jit(solution)/shard_map/reduce_scatter | solution.py:284
  968.0 66.1 %reduce-scatter.24.cloned.1.call-done = f32[96,192]{1,0:T(8,128)} async-done(((f32[768,192]{1,0:T(8,128)}), f32[96,192]{1,0:T(8,128)}) %reduce-scatter.24.cloned.1.call-update) | async-done | bytes 73744 | tf_op jit(solution)/shard_map/reduce_scatter | solution.py:282
  1034.1 65.0 %reduce-scatter.26.cloned.1.call-done = f32[96,128]{1,0:T(8,128)} async-done(((f32[768,128]{1,0:T(8,128)}), f32[96,128]{1,0:T(8,128)}) %reduce-scatter.26.cloned.1.call-update) | async-done | bytes 49168 | tf_op jit(solution)/shard_map/reduce_scatter | solution.py:283
  1099.1 72.5 %reduce-scatter.32.cloned.1.call-done = f32[96,768]{1,0:T(8,128)} async-done(((f32[768,768]{1,0:T(8,128)}), f32[96,768]{1,0:T(8,128)}) %reduce-scatter.32.cloned.1.call-update) | async-done | bytes 294928 | tf_op jit(solution)/shard_map/reduce_scatter | solution.py:286
  1171.6 72.7 %reduce-scatter.30.cloned.1.call-done = f32[96,768]{1,0:T(8,128)} async-done(((f32[768,768]{1,0:T(8,128)}), f32[96,768]{1,0:T(8,128)}) %reduce-scatter.30.cloned.1.call-update) | async-done | bytes 294928 | tf_op jit(solution)/shard_map/reduce_scatter | solution.py:285
  (661 shorter events, 303.1 us)
Async XLA Ops:
  7.2 31.2 %copy-start.177 = (bf16[96,2]{0,1:T(2,128)(2,1)S(1)}, bf16[96,2]{0,1:T(2,128)(2,1)}, u32[]{:S(2)}) copy-start(bf16[96,2]{0,1:T(2,128)(2,1)} %param.13) | copy-start | bytes 1156
  7.2 48.1 %copy-start.175 = (f32[22]{0:T(128)S(1)}, f32[22]{0:T(128)}, u32[]{:S(2)}) copy-start(f32[22]{0:T(128)} %param.21) | copy-start | bytes 268
  7.2 48.1 %copy-start.161 = (s32[4096]{0:T(1024)S(1)}, s32[4096]{0:T(1024)}, u32[]{:S(2)}) copy-start(s32[4096]{0:T(1024)} %param.20) | copy-start | bytes 49156
  7.2 48.3 %copy-start.158 = (bf16[96,128]{1,0:T(8,128)(2,1)S(1)}, bf16[96,128]{1,0:T(8,128)(2,1)}, u32[]{:S(2)}) copy-start(bf16[96,128]{1,0:T(8,128)(2,1)} %param.15) | copy-start | bytes 73732
  7.2 81.9 %copy-start.148 = (bf16[96,192]{1,0:T(8,128)(2,1)S(1)}, bf16[96,192]{1,0:T(8,128)(2,1)}, u32[]{:S(2)}) copy-start(bf16[96,192]{1,0:T(8,128)(2,1)} %param.14) | copy-start | bytes 110596
  7.2 115.1 %copy-start.149 = (bf16[96,192]{1,0:T(8,128)(2,1)S(1)}, bf16[96,192]{1,0:T(8,128)(2,1)}, u32[]{:S(2)}) copy-start(bf16[96,192]{1,0:T(8,128)(2,1)} %param.16) | copy-start | bytes 110596
  7.2 152.8 %all-gather.19.cloned.1.call-start = ((), (), s32[]{:S(2)}) async-start(), calls=%async_computation.18 | async-start | bytes 3932160 | tf_op jit(solution)/shard_map/all_gather | solution.py:155
  9.9 155.6 %all-gather.17.cloned.1.call-start = ((), (), s32[]{:S(2)}) async-start(), calls=%async_computation.17 | async-start | bytes 3932160 | tf_op jit(solution)/shard_map/all_gather | solution.py:155
  10.7 178.5 %all-gather.21.cloned.1.call-start = ((), (), s32[]{:S(2)}) async-start(), calls=%async_computation.19 | async-start | bytes 3932160 | tf_op jit(solution)/shard_map/all_gather | solution.py:195
  13.4 188.3 %all-gather.23.cloned.1.call-start = ((), (), s32[]{:S(2)}) async-start(), calls=%async_computation.20 | async-start | bytes 3932160 | tf_op jit(solution)/shard_map/all_gather | solution.py:195
  14.0 412.1 %all-gather.13.cloned.1.call-start = ((), (), s32[]{:S(2)}) async-start(), calls=%async_computation.11 | async-start | bytes 1327104 | tf_op jit(solution)/shard_map/all_gather | solution.py:151
  14.6 448.8 %all-gather.15.cloned.1.call-start = ((), (), s32[]{:S(2)}) async-start(), calls=%async_computation.12 | async-start | bytes 1327104 | tf_op jit(solution)/shard_map/all_gather | solution.py:152
  15.2 479.8 %all-reduce.20.cloned.1.call-start = ((), (), s32[]{:S(2)}) async-start(), calls=%async_computation.28 | async-start | bytes 4194304 | tf_op jit(solution)/shard_map/psum | solution.py:240
  15.2 144.8 %copy-start.165 = (f32[8]{0:T(128)}, f32[8]{0:T(128)S(1)}, u32[]{:S(2)}) copy-start(f32[8]{0:T(128)S(1)} %multiply_power_fusion) | copy-start | bytes 100
  15.4 195.1 %copy-start.28 = (pred[512,512]{0,1:T(8,128)(4,1)}, pred[512,512]{0,1:T(8,128)(4,1)S(1)}, u32[]{:S(2)}) copy-start(pred[512,512]{0,1:T(8,128)(4,1)S(1)} %iota_compare_fusion.4) | copy-start | bytes 786436
  38.4 132.8 %copy-start.159 = (f32[768]{0:T(1024)}, f32[768]{0:T(1024)S(1)}, u32[]{:S(2)}) copy-start(f32[768]{0:T(1024)S(1)} %get-tuple-element.84) | copy-start | bytes 9220
  55.5 133.8 %copy-start.162 = (f32[2048]{0:T(1024)}, f32[2048]{0:T(1024)S(1)}, u32[]{:S(2)}) copy-start(f32[2048]{0:T(1024)S(1)} %get-tuple-element.152) | copy-start | bytes 24580
  55.5 146.3 %copy-start.114 = (f32[2048]{0:T(1024)}, f32[2048]{0:T(1024)S(1)}, u32[]{:S(2)}) copy-start(f32[2048]{0:T(1024)S(1)} %get-tuple-element.151) | copy-start | bytes 24580
  89.1 94.3 %copy-start.90 = (f32[2048,8]{0,1:T(8,128)}, f32[2048,8]{0,1:T(8,128)S(1)}, u32[]{:S(2)}) copy-start(f32[2048,8]{0,1:T(8,128)S(1)} %get-tuple-element.159) | copy-start | bytes 196612
  426.0 197.3 %reduce-scatter.34.cloned.1.call-start = ((), (), s32[]{:S(2)}) async-start(), calls=%async_computation.26 | async-start | bytes 442368
  530.4 126.1 %reduce-scatter.36.cloned.1.call-start = ((), (), s32[]{:S(2)}) async-start(), calls=%async_computation.27 | async-start | bytes 442368
  531.4 185.4 %reduce-scatter.16.cloned.1.call-start = ((), (), s32[]{:S(2)}) async-start(), calls=%async_computation.13 | async-start | bytes 7864320 | tf_op jit(solution)/shard_map/reduce_scatter | solution.py:184
  538.0 240.3 %reduce-scatter.18.cloned.1.call-start = ((), (), s32[]{:S(2)}) async-start(), calls=%async_computation.14 | async-start | bytes 7864320 | tf_op jit(solution)/shard_map/reduce_scatter | solution.py:184
  561.0 278.6 %reduce-scatter.22.cloned.1.call-start = ((), (), s32[]{:S(2)}) async-start(), calls=%async_computation.16 | async-start | bytes 7864320 | tf_op jit(solution)/shard_map/reduce_scatter | solution.py:265
  568.3 332.7 %reduce-scatter.20.cloned.1.call-start = ((), (), s32[]{:S(2)}) async-start(), calls=%async_computation.15 | async-start | bytes 7864320 | tf_op jit(solution)/shard_map/reduce_scatter | solution.py:265
  574.7 393.3 %reduce-scatter.28.cloned.1.call-start = ((), (), s32[]{:S(2)}) async-start(), calls=%async_computation.23 | async-start | bytes 884736 | tf_op jit(solution)/shard_map/reduce_scatter | solution.py:284
  581.5 452.6 %reduce-scatter.24.cloned.1.call-start = ((), (), s32[]{:S(2)}) async-start(), calls=%async_computation.21 | async-start | bytes 884736 | tf_op jit(solution)/shard_map/reduce_scatter | solution.py:282
  588.9 510.1 %reduce-scatter.26.cloned.1.call-start = ((), (), s32[]{:S(2)}) async-start(), calls=%async_computation.22 | async-start | bytes 442368 | tf_op jit(solution)/shard_map/reduce_scatter | solution.py:283
  595.7 575.9 %reduce-scatter.32.cloned.1.call-start = ((), (), s32[]{:S(2)}) async-start(), calls=%async_computation.25 | async-start | bytes 2654208 | tf_op jit(solution)/shard_map/reduce_scatter | solution.py:286
  605.9 638.4 %reduce-scatter.30.cloned.1.call-start = ((), (), s32[]{:S(2)}) async-start(), calls=%async_computation.24 | async-start | bytes 2654208 | tf_op jit(solution)/shard_map/reduce_scatter | solution.py:285
  616.9 161.4 %copy-start.40 = (bf16[2,512,768]{2,1,0:T(8,128)(2,1)S(1)}, bf16[2,512,768]{2,1,0:T(8,128)(2,1)}, u32[]{:S(2)}) copy-start(bf16[2,512,768]{2,1,0:T(8,128)(2,1)} %param.11) | copy-start | bytes 4718596
  621.0 280.0 %copy-start.41 = (bf16[2,512,768]{2,1,0:T(8,128)(2,1)S(1)}, bf16[2,512,768]{2,1,0:T(8,128)(2,1)}, u32[]{:S(2)}) copy-start(bf16[2,512,768]{2,1,0:T(8,128)(2,1)} %param.19) | copy-start | bytes 4718596
  (198 other events, 1285.4 us)
Sparse Core Ops, SparseCore 0:
  10.2 31.2 all-gather.18
  43.6 28.4 all-gather.16
  73.7 28.4 all-gather.20
  103.7 28.4 all-gather.22
  134.2 40.9 all-gather.12
  177.3 39.8 all-gather.14
  426.2 50.6 all-reduce.19
  530.5 61.4 reduce-scatter.33
  595.3 61.2 reduce-scatter.35
  658.9 57.8 reduce-scatter.15
  719.4 58.8 reduce-scatter.17
  780.7 58.8 reduce-scatter.21
  842.1 58.8 reduce-scatter.19
  904.8 63.1 reduce-scatter.27
  971.7 62.2 reduce-scatter.23
  1037.7 61.2 reduce-scatter.25
  1103.0 68.5 reduce-scatter.31
  1175.5 68.7 reduce-scatter.29
where the time goes:
time: 1260 us; the launch traced here: 1250 us
  waiting for transfers between devices  614 us (49%)
  matrix products  304 us (24%)
  blocking collectives  148 us (12%)
  other arithmetic  135 us (11%)
  local copies, waits for them, and re-layouts  32.3 us (3%)
  between operations  17.6 us (1%)
    reduce_scatter x2, waiting for transfers between devices, shards(): lax.psum_scatter(branch_sum, 'mp', scatter_dimension=0, tiled=True)  120 us
    reduce_scatter x2, waiting for transfers between devices, shards(): lax.psum_scatter(centered_grad * inverse, 'mp', scatter_dimension=0, tile...  119 us
    reduce_scatter x1, waiting for transfers between devices, shards(): lax.psum_scatter(local_grads[5], 'dp', scatter_dimension=0, tiled=True)  72.7 us
    reduce_scatter x1, waiting for transfers between devices, shards(): lax.psum_scatter(local_grads[6], 'dp', scatter_dimension=0, tiled=True)  72.5 us
    another operation x12, other arithmetic  66.7 us
    reduce_scatter x1, waiting for transfers between devices, shards(): lax.psum_scatter(local_grads[2], 'dp', scatter_dimension=0, tiled=True)  66.1 us
    reduce_scatter x1, waiting for transfers between devices, shards(): lax.psum_scatter(local_grads[3], 'dp', scatter_dimension=0, tiled=True)  65 us
    reduce_scatter x1, waiting for transfers between devices, shards(): lax.psum_scatter(local_grads[4], 'dp', scatter_dimension=0, tiled=True)  63.4 us
  transfers between devices with their start and end apart: 18, of which 10 were waited for; matrix products, arithmetic and copies ran while one was open for 35% of the time, Pallas kernels for 0%

commit v1 on v0

--- a/solution.py
+++ b/solution.py
@@ -10,6 +10,22 @@
 epsilon = 1e-05
 sqrt_half = 0.7071067811865476
 inv_sqrt_two_pi = 0.3989422804014327
+
+
+def ring_gather(x, axis, dim):
+    ways, here, step = (lax.axis_size(axis), lax.axis_index(axis), x.shape[dim])
+    shape = [n * ways if d == dim else n for d, n in enumerate(x.shape)]
+    full = lax.dynamic_update_slice_in_dim(jnp.zeros(shape, x.dtype), x, here * step, axis=dim)
+    going_up = going_down = x
+    for far in range(1, ways // 2 + 1):
+        going_up = lax.ppermute(going_up, axis, [(d, (d + 1) % ways) for d in range(ways)])
+        full = lax.dynamic_update_slice_in_dim(full, going_up, (here - far) % ways * step, axis=dim)
+        if 2 * far < ways:
+            going_down = lax.ppermute(going_down, axis, [(d, (d - 1) % ways) for d in range(ways)])
+            full = lax.dynamic_update_slice_in_dim(
+                full, going_down, (here + far) % ways * step, axis=dim
+            )
+    return full
 
 
 def rotary_tables():
@@ -145,7 +161,7 @@
         gathered = (
             lax.all_gather(norm_gains, "dp", axis=0, tiled=True),
             lax.all_gather(norm_biases, "dp", axis=0, tiled=True),
-            lax.all_gather(w_query, "dp", axis=0, tiled=True),
+            ring_gather(w_query, "dp", 0),
             lax.all_gather(w_keyval, "dp", axis=0, tiled=True),
             lax.all_gather(w_output, "dp", axis=0, tiled=True),
             lax.all_gather(w_up, "dp", axis=0, tiled=True),

time: 1260 us -> 1290 us (1.024)
  starting transfers between devices: 1.12 us -> 16.7 us
    ppermute x0 -> x7, starting transfers between devices: none -> 15.6 us  [the longest x3 12.5 us: ring_gather(): lax.ppermute(going_down, axis, [(d, (d - 1) % ways) for d in range(ways)])]
  transfers between devices with their start and end apart: 18 -> 25, of which waited for: 10 -> 13; matrix products, arithmetic and copies ran while one was open for 35% -> 35% of each run, Pallas kernels for 0% -> 0%
where the time goes in v1:
time: 1290 us; the launch traced here: 1280 us
  waiting for transfers between devices  623 us (48%)
  matrix products  309 us (24%)
  blocking collectives  144 us (11%)
  other arithmetic  139 us (11%)
  local copies, waits for them, and re-layouts  32.3 us (3%)
  between operations  17.6 us (1%)
  starting transfers between devices  16.7 us (1%)
    reduce_scatter x2, waiting for transfers between devices, shards(): lax.psum_scatter(branch_sum, 'mp', scatter_dimension=0, tiled=True)  120 us
    reduce_scatter x2, waiting for transfers between devices, shards(): lax.psum_scatter(centered_grad * inverse, 'mp', scatter_dimension=0, tile...  119 us
    reduce_scatter x1, waiting for transfers between devices, shards(): lax.psum_scatter(local_grads[5], 'dp', scatter_dimension=0, tiled=True)  72.7 us
    reduce_scatter x1, waiting for transfers between devices, shards(): lax.psum_scatter(local_grads[6], 'dp', scatter_dimension=0, tiled=True)  72.5 us
    another operation x12, other arithmetic  70.2 us
    reduce_scatter x1, waiting for transfers between devices, shards(): lax.psum_scatter(local_grads[2], 'dp', scatter_dimension=0, tiled=True)  66 us
    reduce_scatter x1, waiting for transfers between devices, shards(): lax.psum_scatter(local_grads[3], 'dp', scatter_dimension=0, tiled=True)  65 us
    reduce_scatter x1, waiting for transfers between devices, shards(): lax.psum_scatter(local_grads[4], 'dp', scatter_dimension=0, tiled=True)  63.4 us
  transfers between devices with their start and end apart: 25, of which 13 were waited for; matrix products, arithmetic and copies ran while one was open for 35% of the time, Pallas kernels for 0%

profile of v1, /device:TPU:0, one launch (start us, length us, event | category | flops | bytes accessed | tf_op | source)
XLA Modules:
  0.0 1281.6 jit_solution(5229562784572510491)
XLA Ops:
  21.0 33.0 %all_gather.59 = bf16[768,192]{1,0:T(8,128)(2,1)} all-gather(bf16[96,192]{1,0:T(8,128)(2,1)S(1)} %copy-done.121), channel_id=1, replica_groups=mesh['dp'=8,'mp'=4] {'dp'}, dimensions={0}, use_global_device_ids=true | all-gather | bytes 331776 | tf_op jit(solution)/shard_map/all_gather | solution.py:204
  54.0 18.3 %all-gather.4 = bf16[8,96,2]{1,2,0:T(2,128)(2,1)S(1)} all-gather(bf16[1,96,2]{1,2,0:T(2,128)(2,1)S(1)} %bitcast.1078), channel_id=1, replica_groups=mesh['dp'=8,'mp'=4] {'dp'}, dimensions={0}, use_global_device_ids=true | all-gather | bytes 3456 | tf_op jit(solution)/shard_map/all_gather | solution.py:162
  73.0 16.3 %all-gather.5 = bf16[8,96,2]{1,2,0:T(2,128)(2,1)S(1)} all-gather(bf16[1,96,2]{1,2,0:T(2,128)(2,1)S(1)} %bitcast.1079), channel_id=1, replica_groups=mesh['dp'=8,'mp'=4] {'dp'}, dimensions={0}, use_global_device_ids=true | all-gather | bytes 3456 | tf_op jit(solution)/shard_map/all_gather | solution.py:163
  91.7 33.0 %all_gather.26 = bf16[768,192]{1,0:T(8,128)(2,1)} all-gather(bf16[96,192]{1,0:T(8,128)(2,1)S(1)} %copy-done.143), channel_id=1, replica_groups=mesh['dp'=8,'mp'=4] {'dp'}, dimensions={0}, use_global_device_ids=true | all-gather | bytes 331776 | tf_op jit(solution)/shard_map/all_gather | solution.py:166
  129.2 32.9 %all_gather.25 = bf16[768,128]{1,0:T(8,128)(2,1)} all-gather(bf16[96,128]{1,0:T(8,128)(2,1)S(1)} %copy-done.152), channel_id=1, replica_groups=mesh['dp'=8,'mp'=4] {'dp'}, dimensions={0}, use_global_device_ids=true | all-gather | bytes 221184 | tf_op jit(solution)/shard_map/all_gather | solution.py:165
  177.1 6.7 collective-permute-done.6
  259.7 6.4 fusion.142
  296.0 6.7 fusion.13
  307.7 11.7 fusion.126
  319.4 11.3 fusion.127
  342.8 6.3 fusion.281
  360.9 15.2 %fusion.3 = (f32[3,512]{1,0:T(4,128)}, f32[3,512]{1,0:T(4,128)}, f32[2048,512,3]{1,0,2:T(8,128)}) fusion(f32[2048,512,3]{1,0,2:T(8,128)} %copy-done.2, f32[3,512]{1,0:T(4,128)S(1)} %log_add_fusion.4, pred[512,2048]{0,1:T(8,128)(4,1)S(1)} %copy-done.7, f32[2048,512,3]{1,0,2:T(8,128)S(1)} %fusion.296, bf16[1,2048,3,64]{1,3,2,0:T(8,128)(2,1)} %bitcast.1072, ...), kind=kOutput, calls=%fused_computation.9 | convolution fusion | flops 421524480 | bytes 39274496 | tf_op jit(solution)/shard_map/sqhd,skd->shqk/dot_general | solution.py:100
  381.0 18.4 %fusion.84 = (bf16[3,512,2048]{1,2,0:T(8,128)(2,1)S(1)}, f32[3,512]{1,0:T(4,128)S(1)}) fusion(f32[2048,512,3]{1,0,2:T(8,128)} %get-tuple-element.174, f32[2048,512,3]{1,0,2:T(8,128)} %copy-done.2, f32[3,512]{1,0:T(4,128)} %get-tuple-element.76, f32[3,512]{1,0:T(4,128)} %copy-done.129, pred[512,2048]{0,1:T(8,128)(4,1)} %iota_compare_fusion, ...), kind=kLoop, calls=%fused_computation.116 | loop fusion | flops 28310016 | bytes 57696256 | tf_op jit(solution)/shard_map/reshape.130
  399.5 16.0 %fusion.85 = bf16[3,512,2048]{1,2,0:T(8,128)(2,1)} fusion(f32[2048,512,3]{1,0,2:T(8,128)} %fusion.281, f32[2048,512,3]{1,0,2:T(8,128)} %copy-done, f32[3,512]{1,0:T(4,128)S(1)} %get-tuple-element.129, f32[3,512]{1,0:T(4,128)S(1)} %log_add_fusion, pred[512,2048]{0,1:T(8,128)(4,1)S(1)} %copy-done.8), kind=kLoop, calls=%fused_computation.117 | loop fusion | flops 15728640 | bytes 32518144 | tf_op jit(solution)/shard_map/reshape.188
  450.8 7.1 fusion.253
  458.1 19.7 %fusion.68 = (bf16[2048,768]{1,0:T(8,128)(2,1)}, f32[2048,768]{1,0:T(8,128)}) fusion(bf16[768,768]{1,0:T(8,128)(2,1)} %all-gather.13.cloned.1.call-done, bf16[1,2048,768]{2,1,0:T(8,128)(2,1)} %all-gather.17.cloned.1.call-done, f32[768]{0:T(1024)} %get-tuple-element.87, f32[768]{0:T(1024)} %get-tuple-element.85, f32[2048]{0:T(1024)} %copy-done.139, ...), kind=kOutput, calls=%fused_computation.100 | convolution fusion | flops 2527592448 | bytes 13785088 | tf_op jit(solution)/shard_map/dot_general | solution.py:195
  477.8 17.9 %fusion.71 = (bf16[2048,768]{1,0:T(8,128)(2,1)}, f32[2048,768]{1,0:T(8,128)}) fusion(bf16[768,768]{1,0:T(8,128)(2,1)S(1)} %copy-done.174, bf16[1,2048,768]{2,1,0:T(8,128)(2,1)S(1)} %copy-done.15, f32[2048]{0:T(1024)S(1)} %copy-done.136, f32[2048]{0:T(1024)S(1)} %copy-done.123, f32[768]{0:T(1024)S(1)} %copy-done.166, f32[768]{0:T(1024)S(1)} %copy-done.162), kind=kOutput, calls=%fused_computation.103 | convolution fusion | flops 2527592448 | bytes 13785088 | tf_op jit(solution)/shard_map/dot_general | solution.py:195
  495.7 7.6 fusion.77
  532.3 11.5 fusion.357
  544.0 7.3 fusion.354
  551.4 10.3 all-reduce.16
  563.8 6.4 convolution_add_fusion.1
  657.2 29.8 %reduce-scatter.36.cloned.1.call-done = f32[96,2]{1,0:T(8,128)} async-done(((f32[768,2]{1,0:T(8,128)}), f32[96,2]{1,0:T(8,128)}) %reduce-scatter.36.cloned.1.call-update) | async-done | bytes 784
  688.4 58.9 %reduce-scatter.16.cloned.1.call-done = f32[512,768]{1,0:T(8,128)} async-done(((f32[2048,768]{1,0:T(8,128)}), f32[512,768]{1,0:T(8,128)}) %reduce-scatter.16.cloned.1.call-update) | async-done | bytes 1572880 | tf_op jit(solution)/shard_map/reduce_scatter | solution.py:200
  747.3 61.4 %reduce-scatter.18.cloned.1.call-done = f32[512,768]{1,0:T(8,128)} async-done(((f32[2048,768]{1,0:T(8,128)}), f32[512,768]{1,0:T(8,128)}) %reduce-scatter.18.cloned.1.call-update) | async-done | bytes 1572880 | tf_op jit(solution)/shard_map/reduce_scatter | solution.py:200
  812.2 57.8 %reduce-scatter.22.cloned.1.call-done = f32[512,768]{1,0:T(8,128)} async-done(((f32[2048,768]{1,0:T(8,128)}), f32[512,768]{1,0:T(8,128)}) %reduce-scatter.22.cloned.1.call-update) | async-done | bytes 1572880 | tf_op jit(solution)/shard_map/reduce_scatter | solution.py:281
  869.9 61.4 %reduce-scatter.20.cloned.1.call-done = f32[512,768]{1,0:T(8,128)} async-done(((f32[2048,768]{1,0:T(8,128)}), f32[512,768]{1,0:T(8,128)}) %reduce-scatter.20.cloned.1.call-update) | async-done | bytes 1572880 | tf_op jit(solution)/shard_map/reduce_scatter | solution.py:281
  935.0 63.4 %reduce-scatter.28.cloned.1.call-done = f32[96,192]{1,0:T(8,128)} async-done(((f32[768,192]{1,0:T(8,128)}), f32[96,192]{1,0:T(8,128)}) %reduce-scatter.28.cloned.1.call-update) | async-done | bytes 73744 | tf_op jit(solution)/shard_map/reduce_scatter | solution.py:300
  998.3 66.0 %reduce-scatter.24.cloned.1.call-done = f32[96,192]{1,0:T(8,128)} async-done(((f32[768,192]{1,0:T(8,128)}), f32[96,192]{1,0:T(8,128)}) %reduce-scatter.24.cloned.1.call-update) | async-done | bytes 73744 | tf_op jit(solution)/shard_map/reduce_scatter | solution.py:298
  1064.3 65.0 %reduce-scatter.26.cloned.1.call-done = f32[96,128]{1,0:T(8,128)} async-done(((f32[768,128]{1,0:T(8,128)}), f32[96,128]{1,0:T(8,128)}) %reduce-scatter.26.cloned.1.call-update) | async-done | bytes 49168 | tf_op jit(solution)/shard_map/reduce_scatter | solution.py:299
  1129.3 72.5 %reduce-scatter.32.cloned.1.call-done = f32[96,768]{1,0:T(8,128)} async-done(((f32[768,768]{1,0:T(8,128)}), f32[96,768]{1,0:T(8,128)}) %reduce-scatter.32.cloned.1.call-update) | async-done | bytes 294928 | tf_op jit(solution)/shard_map/reduce_scatter | solution.py:302
  1201.9 72.7 %reduce-scatter.30.cloned.1.call-done = f32[96,768]{1,0:T(8,128)} async-done(((f32[768,768]{1,0:T(8,128)}), f32[96,768]{1,0:T(8,128)}) %reduce-scatter.30.cloned.1.call-update) | async-done | bytes 294928 | tf_op jit(solution)/shard_map/reduce_scatter | solution.py:301
  (672 shorter events, 335.4 us)
Async XLA Ops:
  7.2 121.9 %copy-start.152 = (bf16[96,128]{1,0:T(8,128)(2,1)S(1)}, bf16[96,128]{1,0:T(8,128)(2,1)}, u32[]{:S(2)}) copy-start(bf16[96,128]{1,0:T(8,128)(2,1)} %param.15) | copy-start | bytes 73732
  7.2 177.3 %all-gather.19.cloned.1.call-start = ((), (), s32[]{:S(2)}) async-start(), calls=%async_computation.18 | async-start | bytes 3932160 | tf_op jit(solution)/shard_map/all_gather | solution.py:171
  9.9 180.2 %all-gather.17.cloned.1.call-start = ((), (), s32[]{:S(2)}) async-start(), calls=%async_computation.17 | async-start | bytes 3932160 | tf_op jit(solution)/shard_map/all_gather | solution.py:171
  10.7 203.1 %all-gather.21.cloned.1.call-start = ((), (), s32[]{:S(2)}) async-start(), calls=%async_computation.19 | async-start | bytes 3932160 | tf_op jit(solution)/shard_map/all_gather | solution.py:211
  13.4 212.8 %all-gather.23.cloned.1.call-start = ((), (), s32[]{:S(2)}) async-start(), calls=%async_computation.20 | async-start | bytes 3932160 | tf_op jit(solution)/shard_map/all_gather | solution.py:211
  14.0 444.0 %all-gather.13.cloned.1.call-start = ((), (), s32[]{:S(2)}) async-start(), calls=%async_computation.11 | async-start | bytes 1327104 | tf_op jit(solution)/shard_map/all_gather | solution.py:167
  14.6 481.1 %all-gather.15.cloned.1.call-start = ((), (), s32[]{:S(2)}) async-start(), calls=%async_computation.12 | async-start | bytes 1327104 | tf_op jit(solution)/shard_map/all_gather | solution.py:168
  14.7 147.4 %collective-permute-start = (bf16[96,192]{1,0:T(8,128)(2,1)S(1)}, bf16[96,192]{1,0:T(8,128)(2,1)S(1)}, u32[]{:S(2)}, u32[]{:S(2)}) collective-permute-start(bf16[96,192]{1,0:T(8,128)(2,1)S(1)} %copy-done.121), channel_id=1, source_target_pairs={{0,4},{4,8},{8,12},{12,16},{16,20},{20,24},{24,28},{28,0},{1,5},{5... | collective-permute-start | bytes 110600 | tf_op jit(solution)/shard_map/ppermute | solution.py:21
  17.7 144.5 %collective-permute-start.1 = (bf16[96,192]{1,0:T(8,128)(2,1)S(1)}, bf16[96,192]{1,0:T(8,128)(2,1)S(1)}, u32[]{:S(2)}, u32[]{:S(2)}) collective-permute-start(bf16[96,192]{1,0:T(8,128)(2,1)S(1)} %copy-done.121), channel_id=1, source_target_pairs={{0,28},{4,0},{8,4},{12,8},{16,12},{20,16},{24,20},{28,24},{1,29},{... | collective-permute-start | bytes 110600 | tf_op jit(solution)/shard_map/ppermute | solution.py:24
  20.8 506.4 %all-reduce.20.cloned.1.call-start = ((), (), s32[]{:S(2)}) async-start(), calls=%async_computation.28 | async-start | bytes 4194304 | tf_op jit(solution)/shard_map/psum | solution.py:256
  21.0 214.0 %copy-start.27 = (pred[512,512]{0,1:T(8,128)(4,1)}, pred[512,512]{0,1:T(8,128)(4,1)S(1)}, u32[]{:S(2)}) copy-start(pred[512,512]{0,1:T(8,128)(4,1)S(1)} %iota_compare_fusion.4) | copy-start | bytes 786436
  73.0 122.7 %copy-start.153 = (f32[768]{0:T(1024)}, f32[768]{0:T(1024)S(1)}, u32[]{:S(2)}) copy-start(f32[768]{0:T(1024)S(1)} %get-tuple-element.84) | copy-start | bytes 9220
  90.7 135.6 %copy-start.109 = (f32[2048]{0:T(1024)}, f32[2048]{0:T(1024)S(1)}, u32[]{:S(2)}) copy-start(f32[2048]{0:T(1024)S(1)} %get-tuple-element.151) | copy-start | bytes 24580
  91.7 116.2 %copy-start.85 = (f32[2048,8]{0,1:T(8,128)}, f32[2048,8]{0,1:T(8,128)S(1)}, u32[]{:S(2)}) copy-start(f32[2048,8]{0,1:T(8,128)S(1)} %get-tuple-element.159) | copy-start | bytes 196612
  162.1 7.7 collective-permute-start.2
  162.2 7.7 collective-permute-start.3
  169.8 7.2 collective-permute-start.4
  169.8 7.2 collective-permute-start.5
  177.0 6.8 collective-permute-start.6
  457.9 197.8 %reduce-scatter.34.cloned.1.call-start = ((), (), s32[]{:S(2)}) async-start(), calls=%async_computation.26 | async-start | bytes 442368
  562.7 124.3 %reduce-scatter.36.cloned.1.call-start = ((), (), s32[]{:S(2)}) async-start(), calls=%async_computation.27 | async-start | bytes 442368
  563.7 183.6 %reduce-scatter.16.cloned.1.call-start = ((), (), s32[]{:S(2)}) async-start(), calls=%async_computation.13 | async-start | bytes 7864320 | tf_op jit(solution)/shard_map/reduce_scatter | solution.py:200
  570.3 238.4 %reduce-scatter.18.cloned.1.call-start = ((), (), s32[]{:S(2)}) async-start(), calls=%async_computation.14 | async-start | bytes 7864320 | tf_op jit(solution)/shard_map/reduce_scatter | solution.py:200
  593.2 276.7 %reduce-scatter.22.cloned.1.call-start = ((), (), s32[]{:S(2)}) async-start(), calls=%async_computation.16 | async-start | bytes 7864320 | tf_op jit(solution)/shard_map/reduce_scatter | solution.py:281
  600.6 330.8 %reduce-scatter.20.cloned.1.call-start = ((), (), s32[]{:S(2)}) async-start(), calls=%async_computation.15 | async-start | bytes 7864320 | tf_op jit(solution)/shard_map/reduce_scatter | solution.py:281
  607.0 391.4 %reduce-scatter.28.cloned.1.call-start = ((), (), s32[]{:S(2)}) async-start(), calls=%async_computation.23 | async-start | bytes 884736 | tf_op jit(solution)/shard_map/reduce_scatter | solution.py:300
  613.7 450.6 %reduce-scatter.24.cloned.1.call-start = ((), (), s32[]{:S(2)}) async-start(), calls=%async_computation.21 | async-start | bytes 884736 | tf_op jit(solution)/shard_map/reduce_scatter | solution.py:298
  621.2 508.1 %reduce-scatter.26.cloned.1.call-start = ((), (), s32[]{:S(2)}) async-start(), calls=%async_computation.22 | async-start | bytes 442368 | tf_op jit(solution)/shard_map/reduce_scatter | solution.py:299
  628.0 573.8 %reduce-scatter.32.cloned.1.call-start = ((), (), s32[]{:S(2)}) async-start(), calls=%async_computation.25 | async-start | bytes 2654208 | tf_op jit(solution)/shard_map/reduce_scatter | solution.py:302
  638.2 636.3 %reduce-scatter.30.cloned.1.call-start = ((), (), s32[]{:S(2)}) async-start(), calls=%async_computation.24 | async-start | bytes 2654208 | tf_op jit(solution)/shard_map/reduce_scatter | solution.py:301
  649.3 159.4 %copy-start.36 = (bf16[2,512,768]{2,1,0:T(8,128)(2,1)S(1)}, bf16[2,512,768]{2,1,0:T(8,128)(2,1)}, u32[]{:S(2)}) copy-start(bf16[2,512,768]{2,1,0:T(8,128)(2,1)} %param.11) | copy-start | bytes 4718596
  653.3 278.0 %copy-start.37 = (bf16[2,512,768]{2,1,0:T(8,128)(2,1)S(1)}, bf16[2,512,768]{2,1,0:T(8,128)(2,1)}, u32[]{:S(2)}) copy-start(bf16[2,512,768]{2,1,0:T(8,128)(2,1)} %param.19) | copy-start | bytes 4718596
  (199 other events, 1837.7 us)
Sparse Core Ops, SparseCore 0:
  10.2 31.2 all-gather.18
  43.6 28.4 all-gather.16
  73.7 28.4 all-gather.20
  103.7 28.4 all-gather.22
  134.2 42.2 all-gather.12
  178.5 39.8 all-gather.14
  458.0 48.4 all-reduce.19
  562.8 59.6 reduce-scatter.33
  625.7 61.2 reduce-scatter.35
  689.3 57.8 reduce-scatter.15
  749.8 58.8 reduce-scatter.17
  811.0 58.8 reduce-scatter.21
  872.5 58.8 reduce-scatter.19
  935.1 63.1 reduce-scatter.27
  1002.0 62.2 reduce-scatter.23
  1068.0 61.2 reduce-scatter.25
  1133.2 68.5 reduce-scatter.31
  1205.8 68.6 reduce-scatter.29
